TPU v7x, 512 devices: a whole 4x4x16 slice. The times are simulated.
512 devices in a mesh: seq: 16 (over x, z_hi), kvh: 8 (over y, core), rep: 4 (over z_lo).
Axes of the slice: x: 4, y: 4, z: 16 (z_hi: 4, z_lo: 4; z = z_hi * 4 + z_lo), core: 2. Of those that a mesh axis runs over, the one named last changes fastest.
Arguments:
- queries: bfloat16 [32, 8, 16, 128], P('rep', 'kvh'), parts along dimension 0, may hold values from -6 to 6
- slot_key_cache: bfloat16 [32, 8, 4096, 128], P('rep', 'kvh', 'seq'), parts along dimension 0, may hold values from -6 to 6
- slot_value_cache: bfloat16 [32, 8, 4096, 128], P('rep', 'kvh', 'seq'), parts along dimension 0, may hold values from -24 to 24
- lengths: int32 [32], P('rep'), parts along dimension 0, may hold values from 512 to 4096, as said below
- output_weight_matrix: bfloat16 [8, 16, 128, 8192], P('kvh', 'seq'), may hold values from -0.125 to 0.125
- residual: float32 [32, 8192], P('rep', ('seq', 'kvh')), parts along dimension 0, may hold values from -6 to 6
Outputs:
- hidden_out: float32 [32, 8192], P('rep', ('seq', 'kvh')), parts along dimension 0
There are 4 independent parts, one for each index of `rep`. A program takes and returns all parts, laid end to end along the dimension named above; an argument that names none is the same for every part. Nothing has to cross between parts.
Inputs may be any that keep to these rules, and one draw needn't show every extreme that they name: Some row has 4096 live positions and some row 512; a row's live block count is lengths rounded up to whole blocks of 32.
All inputs are finite; a program needn't handle non-finite values.
Results may differ from a plain program's by a relative error of at most 0.0028.
Values sent between devices are 32-bit elements; how exact they have to be, the bound alone decides.
No kernel may reach another device: no remote copies, remote signals or barrier semaphores. Data moves between devices by JAX's collectives and lax.ppermute only.
A program may use at most 64 MiB of HBM per device.

v0:
```python
import math

import jax
import jax.numpy as jnp
from jax import lax
from jax.sharding import PartitionSpec as P

BLOCK_POSITIONS = 32


def combined_all(value, axis, combine):
    everything = jax.tree.map(lambda part: lax.all_gather(part, axis), value)
    first = jax.tree.map(lambda part: part[0], everything)

    def step(k, so_far):
        return combine(so_far, jax.tree.map(lambda part: part[k], everything))

    return lax.fori_loop(1, lax.axis_size(axis), step, first)


def join_partials(first, second):
    first_out, first_log = first
    second_out, second_log = second
    highest = jnp.maximum(first_log, second_log)
    first_factor = jnp.exp(first_log - highest)
    second_factor = jnp.exp(second_log - highest)
    denominator = first_factor + second_factor
    joined = (
        first_factor[..., None] * first_out + second_factor[..., None] * second_out
    ) / denominator[..., None]
    return (joined, highest + jnp.log(denominator))


def body(queries, slot_key_cache, slot_value_cache, lengths, output_weight_matrix, residual):
    shard_count = lax.axis_size("seq")
    shard_index = lax.axis_index("seq")
    group_query = queries[:, 0]
    key_rows = slot_key_cache[:, 0]
    value_rows = slot_value_cache[:, 0]
    slot_count = key_rows.shape[1]
    head_size = key_rows.shape[2]
    scale = 1.0 / math.sqrt(head_size)
    slot_ids = jnp.arange(slot_count, dtype=jnp.int32)
    positions = (
        slot_ids // BLOCK_POSITIONS * shard_count + shard_index
    ) * BLOCK_POSITIONS + slot_ids % BLOCK_POSITIONS
    visible = positions[None, :] < lengths[:, None]
    scores = (
        jnp.einsum("bgd,bcd->gbc", group_query, key_rows, preferred_element_type=jnp.float32)
        * scale
    )
    scores = jnp.where(visible[None], scores, -1e30)
    maximum = jnp.max(scores, axis=2)
    weights = jnp.exp(scores - maximum[..., None])
    totals = jnp.sum(weights, axis=2)
    rounded = weights.astype(jnp.bfloat16)
    summed = jnp.einsum("gbc,bcd->gbd", rounded, value_rows, preferred_element_type=jnp.float32)
    partial_value = summed / totals[..., None]
    log_sums = maximum + jnp.log(totals)
    joined, joined_log = combined_all((partial_value, log_sums), "seq", join_partials)
    attention_output = lax.dynamic_slice_in_dim(joined, shard_index, 1, 0)[0]
    out_rows = output_weight_matrix[0, 0]
    contrib = jnp.dot(
        attention_output.astype(jnp.bfloat16), out_rows, preferred_element_type=jnp.float32
    )
    reduced = lax.psum_scatter(contrib, ("seq", "kvh"), scatter_dimension=1, tiled=True)
    return residual + reduced


def solution(mesh):
    in_specs = (
        P("rep", "kvh", None, None),
        P("rep", "kvh", "seq", None),
        P("rep", "kvh", "seq", None),
        P("rep"),
        P("kvh", "seq", None, None),
        P("rep", ("seq", "kvh")),
    )
    out_specs = P("rep", ("seq", "kvh"))
    return jax.shard_map(body, mesh=mesh, in_specs=in_specs, out_specs=out_specs, check_vma=False)
```

profile of v0, /device:TPU:64, one launch (start us, length us, event | category | flops | bytes accessed | tf_op | source)
XLA Modules:
  0.0 950.0 jit_solution(455731166080980313)
XLA Ops:
  6.5 0.9 broadcast_compare_fusion
  7.4 1.4 fusion.25
  8.8 0.2 fusion.10
  9.0 1.9 fusion.7
  11.0 56.9 %all-gather.2 = f32[16,16,8]{1,2,0:T(8,128)S(1)} all-gather(f32[1,16,8]{1,2,0:T(8,128)S(1)} %add_bitcast_fusion), channel_id=3, replica_groups=mesh['seq'=16,'kvh'=8,'rep'=4] {'seq'}, dimensions={0}, use_global_device_ids=true | all-gather | bytes 8704 | tf_op jit(solution)/shard_map/all_gather | solution.py:12
  67.9 32.7 %all-gather.5.cloned.1.call-done = f32[256,8,128]{2,0,1:T(8,128)} async-done(((f32[16,8,128]{2,0,1:T(8,128)}), f32[256,8,128]{2,0,1:T(8,128)}) %all-gather.5.cloned.1.call-update) | async-done | bytes 1048592 | tf_op jit(solution)/shard_map/all_gather | solution.py:12
  100.6 0.8 slice.11
  101.4 18.7 %while.17 = (s32[]{:T(128)}, f32[16,8,128]{2,1,0:T(8,128)S(1)}, f32[16,8]{0,1:T(8,128)S(1)}, f32[16,16,8]{1,2,0:T(8,128)S(1)}, f32[16,16,8,128]{3,1,0,2:T(8,128)}, /*index=5*/s32[]{:T(128)}, s32[]{:T(128)}, s32[]{:T(128)}) while((s32[]{:T(128)}, f32[16,8,128]{2,1,0:T(8,128)S(1)}, f32[16,8]{0,1:T(8,128)S(1)}, f32[16,16,8]{1,2,0:T(8,128)S(1)}, ...), condition=%wide.region_3.4_spmd, body=%wide.region_2.3_spmd.sunk | while | flops 66181 | bytes 335487 | solution.py:18
  101.7 0.8 constant_dynamic-slice_fusion.2
  102.9 0.8 constant_dynamic-slice_fusion.2
  103.8 0.1 fusion.27
  104.2 0.8 constant_dynamic-slice_fusion.2
  105.0 0.1 fusion.27
  105.4 0.8 constant_dynamic-slice_fusion.2
  106.3 0.1 fusion.27
  106.7 0.8 constant_dynamic-slice_fusion.2
  107.5 0.1 fusion.27
  107.9 0.8 constant_dynamic-slice_fusion.2
  108.8 0.1 fusion.27
  109.2 0.8 constant_dynamic-slice_fusion.2
  110.4 0.8 constant_dynamic-slice_fusion.2
  111.6 0.8 constant_dynamic-slice_fusion.2
  112.9 0.8 constant_dynamic-slice_fusion.2
  114.1 0.8 constant_dynamic-slice_fusion.2
  115.4 0.8 constant_dynamic-slice_fusion.2
  116.6 0.8 constant_dynamic-slice_fusion.2
  117.9 0.8 constant_dynamic-slice_fusion.2
  119.1 0.8 constant_dynamic-slice_fusion.2
  120.1 2.9 convolution_bitcast_fusion
  123.0 818.8 %reduce-scatter.4.cloned.1.call-done = f32[64,8]{1,0:T(8,128)} async-done(((f32[8192,8]{1,0:T(8,128)}), f32[64,8]{1,0:T(8,128)}) %reduce-scatter.4.cloned.1.call-update) | async-done | bytes 2064
  941.8 0.8 copy.18
  942.6 0.6 add.124
  (82 shorter events, 5.0 us)
Async XLA Ops:
  6.5 113.6 %copy-start = (bf16[1,1,128,8192]{3,2,1,0:T(8,128)(2,1)S(1)}, bf16[1,1,128,8192]{3,2,1,0:T(8,128)(2,1)}, u32[]{:S(2)}) copy-start(bf16[1,1,128,8192]{3,2,1,0:T(8,128)(2,1)} %param.12) | copy-start | bytes 6291460
  6.5 94.0 %all-gather.5.cloned.1.call-start = ((), (), s32[]{:S(2)}) async-start(), calls=%async_computation.1 | async-start | bytes 1114112 | tf_op jit(solution)/shard_map/all_gather | solution.py:12
  10.9 930.9 %reduce-scatter.4.cloned.1.call-start = ((), (), s32[]{:S(2)}) async-start(), calls=%async_computation.2 | async-start | bytes 4227072
  123.0 819.6 %copy-start.1 = (f32[8,64]{1,0:T(8,128)S(1)}, f32[8,64]{1,0:T(8,128)}, u32[]{:S(2)}) copy-start(f32[8,64]{1,0:T(8,128)} %param.13) | copy-start | bytes 6148
Sparse Core Ops, SparseCore 0:
  11.0 89.4 all-gather.4
  123.1 818.5 reduce-scatter.3
where the time goes:
time: 952 us; the launch traced here: 950 us
  waiting for transfers between devices  851 us (89%)
  blocking collectives  56.9 us (6%)
  local copies, waits for them, and re-layouts  17.6 us (2%)
  between operations  13.4 us (1%)
    unnamed x3, waiting for transfers between devices  819 us
    all_gather x1, blocking collectives, combined_all(): everything = jax.tree.map(lambda part: lax.all_gather(part, axis), value)  56.9 us
    all_gather x1, waiting for transfers between devices, combined_all(): everything = jax.tree.map(lambda part: lax.all_gather(part, axis), value)  32.7 us
  transfers between devices with their start and end apart: 2, of which 2 were waited for; matrix products, arithmetic and copies ran while one was open for 0% of the time, Pallas kernels for 0%

commit v1 on v0

--- a/solution.py
+++ b/solution.py
@@ -6,29 +6,6 @@
 from jax.sharding import PartitionSpec as P
 
 BLOCK_POSITIONS = 32
-
-
-def combined_all(value, axis, combine):
-    everything = jax.tree.map(lambda part: lax.all_gather(part, axis), value)
-    first = jax.tree.map(lambda part: part[0], everything)
-
-    def step(k, so_far):
-        return combine(so_far, jax.tree.map(lambda part: part[k], everything))
-
-    return lax.fori_loop(1, lax.axis_size(axis), step, first)
-
-
-def join_partials(first, second):
-    first_out, first_log = first
-    second_out, second_log = second
-    highest = jnp.maximum(first_log, second_log)
-    first_factor = jnp.exp(first_log - highest)
-    second_factor = jnp.exp(second_log - highest)
-    denominator = first_factor + second_factor
-    joined = (
-        first_factor[..., None] * first_out + second_factor[..., None] * second_out
-    ) / denominator[..., None]
-    return (joined, highest + jnp.log(denominator))
 
 
 def body(queries, slot_key_cache, slot_value_cache, lengths, output_weight_matrix, residual):
@@ -56,15 +33,21 @@
     rounded = weights.astype(jnp.bfloat16)
     summed = jnp.einsum("gbc,bcd->gbd", rounded, value_rows, preferred_element_type=jnp.float32)
     partial_value = summed / totals[..., None]
-    log_sums = maximum + jnp.log(totals)
-    joined, joined_log = combined_all((partial_value, log_sums), "seq", join_partials)
-    attention_output = lax.dynamic_slice_in_dim(joined, shard_index, 1, 0)[0]
+    log_sums = jnp.broadcast_to((maximum + jnp.log(totals))[..., None], partial_value.shape)
+    sent = jnp.concatenate([partial_value, log_sums], axis=1)
+    got = lax.all_to_all(sent, "seq", 0, 0, tiled=True)
+    rows = partial_value.shape[1]
+    logs = got[:, rows:]
+    factors = jnp.exp(logs - jnp.max(logs, axis=0))
+    attention_output = jnp.sum(factors * got[:, :rows], axis=0) / jnp.sum(factors, axis=0)
     out_rows = output_weight_matrix[0, 0]
     contrib = jnp.dot(
         attention_output.astype(jnp.bfloat16), out_rows, preferred_element_type=jnp.float32
     )
-    reduced = lax.psum_scatter(contrib, ("seq", "kvh"), scatter_dimension=1, tiled=True)
-    return residual + reduced
+    width = residual.shape[1]
+    pieces = contrib.reshape(rows, -1, width).transpose(1, 0, 2)
+    exchanged = lax.all_to_all(pieces, ("seq", "kvh"), 0, 0, tiled=True)
+    return residual + jnp.sum(exchanged, axis=0)
 
 
 def solution(mesh):

time: 952 us -> 77.3 us (0.08)
  the two profiles are of different devices: /device:TPU:64 before, /device:TPU:32 now
where the time goes in v1:
time: 77.3 us; the launch traced here: 76.9 us
  blocking collectives  32.9 us (43%)
  starting transfers between devices  16.8 us (22%)
  waiting for transfers between devices  15 us (19%)
  local copies, waits for them, and re-layouts  5.48 us (7%)
  matrix products  3.57 us (5%)
  other arithmetic  3.05 us (4%)
    all_to_all x1, blocking collectives, body(): exchanged = lax.all_to_all(pieces, ('seq', 'kvh'), 0, 0, tiled=True)  32.9 us
    all_to_all x1, starting transfers between devices, body(): got = lax.all_to_all(sent, 'seq', 0, 0, tiled=True)  16.8 us
    all_to_all x1, waiting for transfers between devices, body(): got = lax.all_to_all(sent, 'seq', 0, 0, tiled=True)  15 us
    unnamed x7, local copies, waits for them, and re-layouts  3.95 us
  transfers between devices with their start and end apart: 1, of which 1 were waited for; matrix products, arithmetic and copies ran while one was open for 4% of the time, Pallas kernels for 0%

profile of v1, /device:TPU:32, one launch (start us, length us, event | category | flops | bytes accessed | tf_op | source)
XLA Modules:
  0.0 76.9 jit_solution(15107745057066621342)
XLA Ops:
  0.0 0.0 copy-start
  0.0 0.8 %broadcast_compare_fusion = pred[8,256]{1,0:T(8,128)(4,1)S(1)} fusion(s32[256]{0:T(256)S(1)} %fusion.20, s32[8]{0:T(128)} %param.9), kind=kLoop, calls=%fused_computation.23 | loop fusion | flops 2048 | bytes 3104 | tf_op jit(solution)/shard_map/lt | solution.py:24
  0.8 0.3 copy-done
  1.1 1.1 %fusion.24 = (f32[16,8]{0,1:T(8,128)S(1)}, f32[16,8,256]{2,0,1:T(8,128)S(1)}) fusion(bf16[8,1,16,128]{3,2,1,0:T(8,128)(2,1)} %param.6, bf16[8,1,256,128]{3,2,1,0:T(8,128)(2,1)S(1)} %copy-done, pred[8,256]{1,0:T(8,128)(4,1)S(1)} %broadcast_compare_fusion), kind=kOutput, calls=%fused_computation.36 | convolution fusion | flops 8486784 | bytes 690688 | tf_op jit(solution)/shard_map/bgd,bcd->gbc/dot_general | solution.py:26
  2.1 0.2 fusion.10
  2.3 1.3 %fusion.7 = f32[16,8,128]{2,0,1:T(8,128)S(1)} fusion(bf16[8,1,256,128]{3,2,1,0:T(8,128)(2,1)} %param.8, f32[16,8,256]{2,0,1:T(8,128)S(1)} %get-tuple-element.8, f32[16,8]{0,1:T(8,128)S(1)} %get-tuple-element.7, f32[16,8]{0,1:T(8,128)S(1)} %fusion.10), kind=kOutput, calls=%fused_computation.7 | convolution fusion | flops 8470528 | bytes 721920 | tf_op jit(solution)/shard_map/gbc,bcd->gbd/dot_general | solution.py:34
  3.6 0.1 broadcast_in_dim.16
  3.7 0.7 copy.24
  4.4 16.8 %all-to-all-start = ((f32[16,16,128]{2,1,0:T(8,128)}), f32[16,16,128]{2,1,0:T(8,128)S(1)}, u32[]{:S(2)}, u32[]{:S(2)}) async-start(f32[16,16,128]{2,1,0:T(8,128)} %copy.24), calls=%async_computation | async-start | bytes 262144 | tf_op jit(solution)/shard_map/all_to_all | solution.py:38
  21.2 3.2 %copy.25 = bf16[1,1,128,8192]{2,3,1,0:T(8,128)(2,1)S(1)} copy(bf16[1,1,128,8192]{3,2,1,0:T(8,128)(2,1)} %param.10) | data formatting | bytes 4194304 | tf_op args[4]
  24.4 15.0 %all-to-all-done = f32[16,16,128]{2,1,0:T(8,128)S(1)} async-done(((f32[16,16,128]{2,1,0:T(8,128)}), f32[16,16,128]{2,1,0:T(8,128)S(1)}, u32[]{:S(2)}, u32[]{:S(2)}) %all-to-all-start) | async-done | bytes 131104 | tf_op jit(solution)/shard_map/all_to_all | solution.py:38
  39.5 1.2 %fusion.2 = f32[128,8,64]{0,1,2:T(8,128)S(1)} fusion(bf16[128,64,128]{2,1,0:T(8,128)(2,1)S(1)} %bitcast.29, f32[8,128]{1,0:T(8,128)S(1)} %get-tuple-element.6, f32[8,128]{1,0:T(8,128)S(1)} %get-tuple-element.5), kind=kOutput, calls=%fused_computation.2 | convolution fusion | flops 16779264 | bytes 2367488 | tf_op jit(solution)/shard_map/dot_general | solution.py:44
  40.7 0.0 copy-start.1
  40.7 0.3 copy.27
  41.0 0.3 reshape.62
  41.3 32.9 %all_to_all.10 = f32[128,1,512]{2,1,0:T(1,128)S(1)} all-to-all(f32[128,1,512]{2,1,0:T(1,128)S(1)} %reshape.62), channel_id=1, replica_groups=mesh['seq'=16,'kvh'=8,'rep'=4] {'seq','kvh'}, dimensions={0} | all-to-all | bytes 524288 | tf_op jit(solution)/shard_map/all_to_all | solution.py:49
  74.2 0.5 broadcast.88
  74.7 1.3 %reduce = f32[128,512]{1,0:T(8,128)S(1)} reduce(f32[128,1,512]{2,1,0:T(1,128)S(1)} %all_to_all.10, f32[]{:T(128)} %broadcast.88), dimensions={1}, to_apply=%all_to_all.7.reduce_sub_computation | reduce | bytes 524292 | tf_op jit(solution)/shard_map/all_to_all | solution.py:49
  76.0 0.1 reshape.63
  76.1 0.1 reduce_sum.39
  76.3 0.0 copy-done.1
  76.3 0.6 add.47
  (5 shorter events, 0.1 us)
Async XLA Ops:
  0.0 1.1 %copy-start = (bf16[8,1,256,128]{3,2,1,0:T(8,128)(2,1)S(1)}, bf16[8,1,256,128]{3,2,1,0:T(8,128)(2,1)}, u32[]{:S(2)}) copy-start(bf16[8,1,256,128]{3,2,1,0:T(8,128)(2,1)} %param.7) | copy-start | bytes 1572868
  4.4 35.0 %all-to-all-start = ((f32[16,16,128]{2,1,0:T(8,128)}), f32[16,16,128]{2,1,0:T(8,128)S(1)}, u32[]{:S(2)}, u32[]{:S(2)}) async-start(f32[16,16,128]{2,1,0:T(8,128)} %copy.24), calls=%async_computation | async-start | bytes 262144 | tf_op jit(solution)/shard_map/all_to_all | solution.py:38
  40.7 35.6 %copy-start.1 = (f32[8,64]{1,0:T(8,128)S(1)}, f32[8,64]{1,0:T(8,128)}, u32[]{:S(2)}) copy-start(f32[8,64]{1,0:T(8,128)} %param.11) | copy-start | bytes 6148

commit v2 on v1

v2 whole, which is shorter than its diff:
```python
import math

import jax
import jax.numpy as jnp
from jax import lax
from jax.experimental import pallas as pl
from jax.experimental.pallas import tpu as pltpu
from jax.sharding import Mesh, PartitionSpec as P

BLOCK_POSITIONS = 32
LANES = 128
MEBI = 1 << 20
SEQ = ("x", "z_hi")
KVH = ("y", "core")


def attend_kernel(shards, lengths_ref, query_hbm, key_hbm, value_hbm, matrix_hbm,
                  sent_ref, matrix_ref, query_ref, key_ref, value_ref, query_sem, key_sem, value_sem, matrix_sem):
    rows, groups, size = query_ref.shape
    slots = key_ref.shape[1]
    query_copy = pltpu.make_async_copy(query_hbm, query_ref, query_sem)
    key_copies = [pltpu.make_async_copy(key_hbm.at[b], key_ref.at[b], key_sem.at[b]) for b in range(rows)]
    value_copies = [
        pltpu.make_async_copy(value_hbm.at[b], value_ref.at[b], value_sem.at[b]) for b in range(rows)
    ]
    matrix_copy = pltpu.make_async_copy(matrix_hbm, matrix_ref, matrix_sem)
    query_copy.start()
    for copy in key_copies:
        copy.start()
    for copy in value_copies:
        copy.start()
    matrix_copy.start()
    scale = 1.0 / math.sqrt(size)
    slot_ids = lax.broadcasted_iota(jnp.int32, (groups, slots), 1)
    positions = (
        slot_ids // BLOCK_POSITIONS * shards + lax.axis_index(SEQ)
    ) * BLOCK_POSITIONS + slot_ids % BLOCK_POSITIONS
    query_copy.wait()
    scores = []
    for b in range(rows):
        key_copies[b].wait()
        scores.append(
            lax.dot_general(
                query_ref[b], key_ref[b], (((1,), (1,)), ((), ())), preferred_element_type=jnp.float32
            )
        )
    logs = jnp.zeros((groups, LANES), jnp.float32)
    lane = lax.broadcasted_iota(jnp.int32, (groups, LANES), 1)
    weights = []
    totals = []
    for b in range(rows):
        masked = jnp.where(positions < lengths_ref[b], scores[b] * scale, -1e30)
        top = jnp.max(masked, axis=1, keepdims=True)
        weight = jnp.exp(masked - top)
        total = jnp.sum(weight, axis=1, keepdims=True)
        weights.append(weight.astype(jnp.bfloat16))
        totals.append(total)
        logs = jnp.where(lane == b, top + jnp.log(total), logs)
    for b in range(rows):
        value_copies[b].wait()
        summed = jnp.dot(weights[b], value_ref[b], preferred_element_type=jnp.float32)
        sent_ref[pl.ds(b, groups, stride=rows + 1), :] = summed / totals[b]
    sent_ref[pl.ds(rows, groups, stride=rows + 1), :] = logs
    matrix_copy.wait()


def attend(lengths, queries, keys, values, matrix, shards):
    rows, groups, size = queries.shape
    slots = keys.shape[1]
    outside = pl.BlockSpec(memory_space=pltpu.HBM)
    inside = pl.BlockSpec(memory_space=pltpu.VMEM)
    scalars = pl.BlockSpec(memory_space=pltpu.SMEM)
    return pl.pallas_call(
        lambda *refs: attend_kernel(shards, *refs),
        name="attend",
        compiler_params=pltpu.CompilerParams(vmem_limit_bytes=8 * MEBI),
        out_shape=(
            jax.ShapeDtypeStruct((groups * (rows + 1), size), jnp.float32),
            jax.ShapeDtypeStruct(matrix.shape, matrix.dtype),
        ),
        in_specs=[scalars, outside, outside, outside, outside],
        out_specs=(inside, inside),
        scratch_shapes=[
            pltpu.VMEM((rows, groups, size), queries.dtype),
            pltpu.VMEM((rows, slots, size), keys.dtype),
            pltpu.VMEM((rows, slots, size), values.dtype),
            pltpu.SemaphoreType.DMA,
            pltpu.SemaphoreType.DMA((rows,)),
            pltpu.SemaphoreType.DMA((rows,)),
            pltpu.SemaphoreType.DMA,
        ],
    )(*[pltpu.with_memory_space_constraint(a, pltpu.HBM) for a in (lengths, queries, keys, values, matrix)])


def project_kernel(order, got_ref, weight_ref, out_ref):
    pieces, rows, lanes = out_ref.shape
    shards = got_ref.shape[0] // (rows + 1)
    logs = got_ref[pl.ds(rows, shards, stride=rows + 1), :]
    factors = jnp.exp(logs - jnp.max(logs, axis=0, keepdims=True))
    factors = factors / jnp.sum(factors, axis=0, keepdims=True)
    diagonal = lax.broadcasted_iota(jnp.int32, (rows, lanes), 0) == lax.broadcasted_iota(
        jnp.int32, (rows, lanes), 1
    )
    attended = jnp.zeros((rows, lanes), jnp.float32)
    for s in range(shards):
        factor = jnp.sum(
            jnp.where(diagonal, factors[s : s + 1, :], 0.0), axis=1, keepdims=True
        )
        attended += factor * got_ref[pl.ds(s * (rows + 1), rows), :]
    attended = attended.astype(jnp.bfloat16)
    step = 8
    for first in range(0, pieces, step):
        product = jnp.dot(
            attended,
            weight_ref[:, first * lanes : (first + step) * lanes],
            preferred_element_type=jnp.float32,
        )
        for j in range(step):
            out_ref[order[first + j]] = product[:, j * lanes : (j + 1) * lanes]


def project(got, weights, order, rows):
    size, features = weights.shape
    return pl.pallas_call(
        lambda *refs: project_kernel(order, *refs),
        name="project",
        compiler_params=pltpu.CompilerParams(vmem_limit_bytes=8 * MEBI),
        out_shape=jax.ShapeDtypeStruct((features // LANES, rows, LANES), jnp.float32),
        in_specs=[pl.BlockSpec(memory_space=pltpu.VMEM)] * 2,
        out_specs=pl.BlockSpec(memory_space=pltpu.VMEM),
    )(got, weights)


def plane_sum_kernel(got_ref, out_ref):
    sources, blocks = got_ref.shape[:2]
    copies = out_ref.shape[0] // blocks
    for i in range(blocks):
        total = got_ref[0, i]
        for s in range(1, sources):
            total += got_ref[s, i]
        for c in range(copies):
            out_ref[i * copies + c] = total


def plane_sum(got, blocks, copies):
    pieces, rows, lanes = got.shape
    return pl.pallas_call(
        plane_sum_kernel,
        name="plane_sum",
        compiler_params=pltpu.CompilerParams(vmem_limit_bytes=2 * MEBI),
        out_shape=jax.ShapeDtypeStruct((blocks * copies, rows, lanes), jnp.float32),
        in_specs=[pl.BlockSpec(memory_space=pltpu.VMEM)],
        out_specs=pl.BlockSpec(memory_space=pltpu.VMEM),
    )(got.reshape(pieces // blocks, blocks, rows, lanes))


def finish_kernel(got_ref, residual_ref, out_ref):
    width = out_ref.shape[1]
    total = got_ref[0]
    for s in range(1, got_ref.shape[0]):
        total += got_ref[s]
    half = jnp.where(lax.axis_index("core") == 0, total[:, :width], total[:, width:])
    out_ref[...] = residual_ref[...] + half


def finish(got, residual):
    return pl.pallas_call(
        finish_kernel,
        name="finish",
        compiler_params=pltpu.CompilerParams(vmem_limit_bytes=2 * MEBI),
        out_shape=jax.ShapeDtypeStruct(residual.shape, jnp.float32),
        in_specs=[pl.BlockSpec(memory_space=pltpu.VMEM)] * 2,
        out_specs=pl.BlockSpec(memory_space=pltpu.VMEM),
    )(got, residual)


def body(queries, slot_key_cache, slot_value_cache, lengths, output_weight_matrix, residual):
    x_size, z_size = lax.axis_size("x"), lax.axis_size("z_hi")
    y_size, cores = lax.axis_size("y"), lax.axis_size("core")
    shards = x_size * z_size
    rows = queries.shape[0]
    sent, matrix = attend(
        lengths,
        queries[:, 0],
        slot_key_cache[:, 0],
        slot_value_cache[:, 0],
        output_weight_matrix[0, 0],
        shards,
    )
    lines, size = sent.shape
    got = lax.all_to_all(sent.reshape(lines, 1, size), SEQ, 0, 0, tiled=True).reshape(lines, size)
    order = [
        (x * y_size + y) * z_size + z
        for x in range(x_size)
        for z in range(z_size)
        for y in range(y_size)
    ]
    pieces = project(got, matrix, order, rows)
    plane = lax.all_to_all(pieces, ("x", "y"), 0, 0, tiled=True)
    blocks = plane_sum(plane, z_size, cores)
    last = lax.all_to_all(blocks, ("z_hi", "core"), 0, 0, tiled=True)
    return finish(last, residual)


def solution(mesh):
    fine = Mesh(
        mesh.devices.reshape(4, mesh.shape["seq"] // 4, mesh.shape["kvh"] // 2, 2, mesh.shape["rep"]),
        ("x", "z_hi", "y", "core", "rep"),
    )
    in_specs = (
        P("rep", KVH, None, None),
        P("rep", KVH, SEQ, None),
        P("rep", KVH, SEQ, None),
        P("rep"),
        P(KVH, SEQ, None, None),
        P("rep", SEQ + KVH),
    )
    out_specs = P("rep", SEQ + KVH)
    return jax.shard_map(body, mesh=fine, in_specs=in_specs, out_specs=out_specs, check_vma=False)
```

time: 77.3 us -> 67.9 us (0.88)
  the two profiles are of different devices: /device:TPU:32 before, /device:TPU:1 now
where the time goes in v2:
time: 67.9 us; the launch traced here: 67.7 us
  blocking collectives  62.1 us (91%)
  Pallas kernels  5.58 us (8%)
    all_to_all x1, blocking collectives, body(): lax.all_to_all(sent.reshape(lines, 1, size), SEQ, 0, 0, tiled=True)  33 us
    all_to_all x1, blocking collectives, body(): last = lax.all_to_all(blocks, ('z_hi', 'core'), 0, 0, tiled=True)  17.4 us
    all_to_all x1, blocking collectives, body(): plane = lax.all_to_all(pieces, ('x', 'y'), 0, 0, tiled=True)  11.7 us
    pallas_call x1, Pallas kernels, attend(): pl.pallas_call(lambda *refs: attend_kernel(shards, *refs), name='attend',...  4.41 us

profile of v2, /device:TPU:1, one launch (start us, length us, event | category | flops | bytes accessed | tf_op | source)
XLA Modules:
  0.0 67.7 jit_solution(11461479895745849579)
XLA Ops:
  0.0 4.4 %attend.1 = (f32[144,128]{1,0:T(8,128)S(1)}, bf16[128,8192]{1,0:T(8,128)(2,1)S(1)}) custom-call(s32[8]{0:T(128)} %refs_0_.1, bf16[8,16,128]{2,1,0:T(8,128)(2,1)} %bitcast.15, bf16[8,256,128]{2,1,0:T(8,128)(2,1)} %bitcast.13, bf16[8,256,128]{2,1,0:T(8,128)(2,1)} %bitcast.14, bf16[128,8192]{1,0:T(8,128)(2,1)} %bitcast.12), custom_call_target="tpu_custom_call" | custom-call | tf_op jit(solution)/shard_map/attend/pallas_call | solution.py:73
  4.4 0.0 copy-start
  4.4 33.0 %all_to_all.15 = f32[144,1,128]{2,1,0:T(1,128)S(1)} all-to-all(f32[144,1,128]{2,1,0:T(1,128)S(1)} %bitcast.11), channel_id=1, replica_groups=mesh['x'=4,'z_hi'=4,'y'=4,'core'=2,'rep'=4] {'x','z_hi'}, dimensions={0} | all-to-all | bytes 147456 | tf_op jit(solution)/shard_map/all_to_all | solution.py:191
  37.4 0.5 project.1
  37.9 11.7 %all_to_all.16 = f32[64,8,128]{2,1,0:T(8,128)S(1)} all-to-all(f32[64,8,128]{2,1,0:T(8,128)S(1)} %project.1), channel_id=1, replica_groups=mesh['x'=4,'z_hi'=4,'y'=4,'core'=2,'rep'=4] {'x','y'}, dimensions={0} | all-to-all | bytes 524288 | tf_op jit(solution)/shard_map/all_to_all | solution.py:199
  49.6 17.4 %all_to_all.17.got_ref = f32[8,8,128]{2,1,0:T(8,128)S(1)} all-to-all(f32[8,8,128]{2,1,0:T(8,128)S(1)} %plane_sum.1), channel_id=1, replica_groups=mesh['x'=4,'z_hi'=4,'y'=4,'core'=2,'rep'=4] {'z_hi','core'}, dimensions={0} | all-to-all | bytes 65536 | tf_op jit(solution)/shard_map/all_to_all | solution.py:201
  67.0 0.0 copy-done
  67.0 0.7 finish.1
  (1 shorter events, 0.0 us)
Async XLA Ops:
  4.4 62.6 %copy-start = (f32[8,64]{1,0:T(8,128)S(1)}, f32[8,64]{1,0:T(8,128)}, u32[]{:S(2)}) copy-start(f32[8,64]{1,0:T(8,128)} %residual_ref.1) | copy-start | bytes 6148

commit v3 on v2

v3 whole, which is shorter than its diff:
```python
import math

import jax
import jax.numpy as jnp
from jax import lax
from jax.experimental import pallas as pl
from jax.experimental.pallas import tpu as pltpu
from jax.sharding import Mesh, PartitionSpec as P

BLOCK_POSITIONS = 32
LANES = 128
MEBI = 1 << 20
SEQ = ("x", "z_hi")
KVH = ("y", "core")


def attend_kernel(shards, lengths_hbm, query_hbm, key_hbm, value_hbm, matrix_hbm, sent_ref, matrix_ref,
                  lengths_ref, query_ref, key_ref, value_ref, sems):
    rows, groups, size = query_ref.shape
    slots = key_ref.shape[1]
    lengths_copy, query_copy, key_copy, value_copy, matrix_copy = [
        pltpu.make_async_copy(source, target, sems.at[i])
        for i, (source, target) in enumerate(
            (
                (lengths_hbm, lengths_ref),
                (query_hbm, query_ref),
                (key_hbm, key_ref),
                (value_hbm, value_ref),
                (matrix_hbm, matrix_ref),
            )
        )
    ]
    lengths_copy.start()
    query_copy.start()
    key_copy.start()
    value_copy.start()
    matrix_copy.start()
    scale = 1.0 / math.sqrt(size)
    slot_ids = lax.broadcasted_iota(jnp.int32, (groups, slots), 1)
    positions = (
        slot_ids // BLOCK_POSITIONS * shards + lax.axis_index(SEQ)
    ) * BLOCK_POSITIONS + slot_ids % BLOCK_POSITIONS
    lane = lax.broadcasted_iota(jnp.int32, (groups, LANES), 1)
    lengths_copy.wait()
    query_copy.wait()
    key_copy.wait()
    scores = [
        lax.dot_general(
            query_ref[b], key_ref[b], (((1,), (1,)), ((), ())), preferred_element_type=jnp.float32
        )
        for b in range(rows)
    ]
    logs = jnp.zeros((groups, LANES), jnp.float32)
    weights = []
    totals = []
    for b in range(rows):
        masked = jnp.where(positions < lengths_ref[b], scores[b] * scale, -1e30)
        top = jnp.max(masked, axis=1, keepdims=True)
        weight = jnp.exp(masked - top)
        total = jnp.sum(weight, axis=1, keepdims=True)
        weights.append(weight.astype(jnp.bfloat16))
        totals.append(total)
        logs = jnp.where(lane == b, top + jnp.log(total), logs)
    value_copy.wait()
    for b in range(rows):
        summed = jnp.dot(weights[b], value_ref[b], preferred_element_type=jnp.float32)
        sent_ref[pl.ds(b, groups, stride=rows + 1), :] = summed / totals[b]
    sent_ref[pl.ds(rows, groups, stride=rows + 1), :] = logs
    matrix_copy.wait()


def attend(lengths, queries, keys, values, matrix, shards):
    rows, groups, size = queries.shape
    outside = pl.BlockSpec(memory_space=pltpu.HBM)
    inside = pl.BlockSpec(memory_space=pltpu.VMEM)
    operands = (lengths, queries, keys, values, matrix)
    return pl.pallas_call(
        lambda *refs: attend_kernel(shards, *refs),
        name="attend",
        compiler_params=pltpu.CompilerParams(vmem_limit_bytes=8 * MEBI),
        out_shape=(
            jax.ShapeDtypeStruct((groups * (rows + 1), size), jnp.float32),
            jax.ShapeDtypeStruct(matrix.shape, matrix.dtype),
        ),
        in_specs=[outside] * len(operands),
        out_specs=(inside, inside),
        scratch_shapes=[pltpu.SMEM(lengths.shape, lengths.dtype)]
        + [pltpu.VMEM(a.shape, a.dtype) for a in (queries, keys, values)]
        + [pltpu.SemaphoreType.DMA((len(operands),))],
    )(*[pltpu.with_memory_space_constraint(a, pltpu.HBM) for a in operands])


def project_kernel(got_ref, weight_ref, out_ref):
    pieces, rows, lanes = out_ref.shape
    shards = got_ref.shape[0] // (rows + 1)
    logs = got_ref[pl.ds(rows, shards, stride=rows + 1), :]
    factors = jnp.exp(logs - jnp.max(logs, axis=0, keepdims=True))
    factors = factors / jnp.sum(factors, axis=0, keepdims=True)
    diagonal = lax.broadcasted_iota(jnp.int32, (rows, lanes), 0) == lax.broadcasted_iota(
        jnp.int32, (rows, lanes), 1
    )
    attended = jnp.zeros((rows, lanes), jnp.float32)
    for s in range(shards):
        factor = jnp.sum(
            jnp.where(diagonal, factors[s : s + 1, :], 0.0), axis=1, keepdims=True
        )
        attended += factor * got_ref[pl.ds(s * (rows + 1), rows), :]
    attended = attended.astype(jnp.bfloat16)
    step = 8
    for first in range(0, pieces, step):
        product = jnp.dot(
            attended,
            weight_ref[:, first * lanes : (first + step) * lanes],
            preferred_element_type=jnp.float32,
        )
        for j in range(step):
            out_ref[first + j] = product[:, j * lanes : (j + 1) * lanes]


def project(got, weights, rows):
    size, features = weights.shape
    return pl.pallas_call(
        project_kernel,
        name="project",
        compiler_params=pltpu.CompilerParams(vmem_limit_bytes=8 * MEBI),
        out_shape=jax.ShapeDtypeStruct((features // LANES, rows, LANES), jnp.float32),
        in_specs=[pl.BlockSpec(memory_space=pltpu.VMEM)] * 2,
        out_specs=pl.BlockSpec(memory_space=pltpu.VMEM),
    )(got, weights)


def core_sum_kernel(got_ref, out_ref):
    pieces, part, lanes = out_ref.shape
    half = lanes // 2
    low = lax.broadcasted_iota(jnp.int32, (part, lanes), 1) < half
    first = lax.axis_index("core") == 0
    for i in range(pieces):
        total = got_ref[0, i] + got_ref[1, i]
        other = pltpu.roll(total, half, 1)
        one = jnp.where(first, total, other)
        two = jnp.where(first, other, total)
        out_ref[i] = jnp.where(low, one[:part], two[part:])


def core_sum(got):
    cores, pieces, rows, lanes = got.shape
    return pl.pallas_call(
        core_sum_kernel,
        name="core_sum",
        compiler_params=pltpu.CompilerParams(vmem_limit_bytes=2 * MEBI),
        out_shape=jax.ShapeDtypeStruct((pieces, rows // cores, lanes), jnp.float32),
        in_specs=[pl.BlockSpec(memory_space=pltpu.VMEM)],
        out_specs=pl.BlockSpec(memory_space=pltpu.VMEM),
    )(got)


def finish_kernel(got_ref, residual_ref, out_ref):
    width = out_ref.shape[1]
    part = got_ref.shape[1]
    totals = [got_ref[s] for s in range(got_ref.shape[0])]
    while len(totals) > 1:
        totals = [totals[i] + totals[i + 1] for i in range(0, len(totals), 2)]
    out_ref[:part] = residual_ref[:part] + totals[0][:, :width]
    out_ref[part:] = residual_ref[part:] + totals[0][:, width:]


def finish(got, residual):
    return pl.pallas_call(
        finish_kernel,
        name="finish",
        compiler_params=pltpu.CompilerParams(vmem_limit_bytes=2 * MEBI),
        out_shape=jax.ShapeDtypeStruct(residual.shape, jnp.float32),
        in_specs=[pl.BlockSpec(memory_space=pltpu.VMEM)] * 2,
        out_specs=pl.BlockSpec(memory_space=pltpu.VMEM),
    )(got, residual)


def body(queries, slot_key_cache, slot_value_cache, lengths, output_weight_matrix, residual):
    shards = lax.axis_size(SEQ)
    rows = queries.shape[0]
    sent, matrix = attend(
        lengths,
        queries[:, 0],
        slot_key_cache[:, 0],
        slot_value_cache[:, 0],
        output_weight_matrix[0, 0],
        shards,
    )
    lines, size = sent.shape
    got = lax.all_to_all(sent.reshape(lines, 1, size), SEQ, 0, 0, tiled=True).reshape(lines, size)
    pieces = project(got, matrix, rows)
    both = lax.all_gather(pieces, "core")
    packed = core_sum(both)
    last = lax.all_to_all(packed, ("x", "z_hi", "y"), 0, 0, tiled=True)
    return finish(last, residual)


def solution(mesh):
    fine = Mesh(
        mesh.devices.reshape(4, mesh.shape["seq"] // 4, mesh.shape["kvh"] // 2, 2, mesh.shape["rep"]),
        ("x", "z_hi", "y", "core", "rep"),
    )
    in_specs = (
        P("rep", KVH, None, None),
        P("rep", KVH, SEQ, None),
        P("rep", KVH, SEQ, None),
        P("rep"),
        P(KVH, SEQ, None, None),
        P("rep", SEQ + KVH),
    )
    out_specs = P("rep", SEQ + KVH)
    return jax.shard_map(body, mesh=fine, in_specs=in_specs, out_specs=out_specs, check_vma=False)
```

time: 67.9 us -> 64.9 us (0.956)
  the two profiles are of different devices: /device:TPU:1 before, /device:TPU:32 now
where the time goes in v3:
time: 64.9 us; the launch traced here: 64.8 us
  blocking collectives  61.5 us (95%)
  Pallas kernels  3.28 us (5%)
    all_to_all x1, blocking collectives, body(): lax.all_to_all(sent.reshape(lines, 1, size), SEQ, 0, 0, tiled=True)  32.7 us
    all_to_all x1, blocking collectives, body(): last = lax.all_to_all(packed, ('x', 'z_hi', 'y'), 0, 0, tiled=True)  26.6 us
    all_gather x1, blocking collectives, body(): both = lax.all_gather(pieces, 'core')  2.19 us
    pallas_call x1, Pallas kernels, attend(): pl.pallas_call(lambda *refs: attend_kernel(shards, *refs), name='attend',...  1.99 us

profile of v3, /device:TPU:32, one launch (start us, length us, event | category | flops | bytes accessed | tf_op | source)
XLA Modules:
  0.0 64.8 jit_solution(16063643806099975697)
XLA Ops:
  0.0 2.0 %attend.1 = (f32[144,128]{1,0:T(8,128)S(1)}, bf16[128,8192]{1,0:T(8,128)(2,1)S(1)}) custom-call(s32[8]{0:T(128)} %refs_0_.1, bf16[8,16,128]{2,1,0:T(8,128)(2,1)} %bitcast.15, bf16[8,256,128]{2,1,0:T(8,128)(2,1)} %bitcast.13, bf16[8,256,128]{2,1,0:T(8,128)(2,1)} %bitcast.14, bf16[128,8192]{1,0:T(8,128)(2,1)} %bitcast.12), custom_call_target="tpu_custom_call" | custom-call | tf_op jit(solution)/shard_map/attend/pallas_call | solution.py:77
  2.0 32.7 %all_to_all.10 = f32[144,1,128]{2,1,0:T(1,128)S(1)} all-to-all(f32[144,1,128]{2,1,0:T(1,128)S(1)} %bitcast.11), channel_id=1, replica_groups=mesh['x'=4,'z_hi'=4,'y'=4,'core'=2,'rep'=4] {'x','z_hi'}, dimensions={0} | all-to-all | bytes 147456 | tf_op jit(solution)/shard_map/all_to_all | solution.py:190
  34.7 0.0 copy-start
  34.7 0.5 project.1
  35.1 2.2 %all-gather = f32[128,8,128]{2,1,0:T(8,128)S(1)} all-gather(f32[64,8,128]{2,1,0:T(8,128)S(1)} %project.1), channel_id=2, replica_groups=mesh['x'=4,'z_hi'=4,'y'=4,'core'=2,'rep'=4] {'core'}, dimensions={0}, use_global_device_ids=true | all-gather | bytes 786432 | tf_op jit(solution)/shard_map/all_gather | solution.py:192
  37.3 0.1 core_sum.1
  37.5 26.6 %all_to_all.11.got_ref = f32[64,4,128]{2,1,0:T(4,128)S(1)} all-to-all(f32[64,4,128]{2,1,0:T(4,128)S(1)} %core_sum.1), channel_id=1, replica_groups=mesh['x'=4,'z_hi'=4,'y'=4,'core'=2,'rep'=4] {'x','z_hi','y'}, dimensions={0} | all-to-all | bytes 262144 | tf_op jit(solution)/shard_map/all_to_all | solution.py:194
  64.1 0.0 copy-done
  64.1 0.7 %finish.1 = f32[8,64]{1,0:T(8,128)} custom-call(f32[64,4,128]{2,1,0:T(4,128)S(1)} %all_to_all.11.got_ref, f32[8,64]{1,0:T(8,128)S(1)} %copy-done), custom_call_target="tpu_custom_call" | custom-call | tf_op jit(solution)/shard_map/finish/pallas_call | solution.py:168
Async XLA Ops:
  34.7 29.4 %copy-start = (f32[8,64]{1,0:T(8,128)S(1)}, f32[8,64]{1,0:T(8,128)}, u32[]{:S(2)}) copy-start(f32[8,64]{1,0:T(8,128)} %residual_ref.1) | copy-start | bytes 6148

commit v4 on v3

--- a/solution.py
+++ b/solution.py
@@ -10,7 +10,8 @@
 BLOCK_POSITIONS = 32
 LANES = 128
 MEBI = 1 << 20
-SEQ = ("x", "z_hi")
+SEQ = ("x", "z1", "z0")
+PEERS = ("z0", "z1", "x", "y")
 KVH = ("y", "core")
 
 
@@ -90,7 +91,7 @@
     )(*[pltpu.with_memory_space_constraint(a, pltpu.HBM) for a in operands])
 
 
-def project_kernel(got_ref, weight_ref, out_ref):
+def project_kernel(places, got_ref, weight_ref, out_ref):
     pieces, rows, lanes = out_ref.shape
     shards = got_ref.shape[0] // (rows + 1)
     logs = got_ref[pl.ds(rows, shards, stride=rows + 1), :]
@@ -114,13 +115,13 @@
             preferred_element_type=jnp.float32,
         )
         for j in range(step):
-            out_ref[first + j] = product[:, j * lanes : (j + 1) * lanes]
-
-
-def project(got, weights, rows):
+            out_ref[places[first + j]] = product[:, j * lanes : (j + 1) * lanes]
+
+
+def project(got, weights, places, rows):
     size, features = weights.shape
     return pl.pallas_call(
-        project_kernel,
+        lambda *refs: project_kernel(places, *refs),
         name="project",
         compiler_params=pltpu.CompilerParams(vmem_limit_bytes=8 * MEBI),
         out_shape=jax.ShapeDtypeStruct((features // LANES, rows, LANES), jnp.float32),
@@ -188,17 +189,25 @@
     )
     lines, size = sent.shape
     got = lax.all_to_all(sent.reshape(lines, 1, size), SEQ, 0, 0, tiled=True).reshape(lines, size)
-    pieces = project(got, matrix, rows)
+    sizes = [lax.axis_size(axis) for axis in PEERS]
+    places = [
+        ((z0 * sizes[1] + z1) * sizes[2] + x) * sizes[3] + y
+        for x in range(sizes[2])
+        for z1 in range(sizes[1])
+        for z0 in range(sizes[0])
+        for y in range(sizes[3])
+    ]
+    pieces = project(got, matrix, places, rows)
     both = lax.all_gather(pieces, "core")
     packed = core_sum(both)
-    last = lax.all_to_all(packed, ("x", "z_hi", "y"), 0, 0, tiled=True)
+    last = lax.all_to_all(packed, PEERS, 0, 0, tiled=True)
     return finish(last, residual)
 
 
 def solution(mesh):
     fine = Mesh(
-        mesh.devices.reshape(4, mesh.shape["seq"] // 4, mesh.shape["kvh"] // 2, 2, mesh.shape["rep"]),
-        ("x", "z_hi", "y", "core", "rep"),
+        mesh.devices.reshape(4, 2, mesh.shape["seq"] // 8, mesh.shape["kvh"] // 2, 2, mesh.shape["rep"]),
+        ("x", "z1", "z0", "y", "core", "rep"),
     )
     in_specs = (
         P("rep", KVH, None, None),

time: 64.9 us -> 63.6 us (0.980)
  the two profiles are of different devices: /device:TPU:32 before, /device:TPU:64 now
where the time goes in v4:
time: 63.6 us; the launch traced here: 63.4 us
  blocking collectives  60.1 us (94%)
  Pallas kernels  3.28 us (5%)
    all_to_all x1, blocking collectives, body(): lax.all_to_all(sent.reshape(lines, 1, size), SEQ, 0, 0, tiled=True)  31.8 us
    all_to_all x1, blocking collectives, body(): last = lax.all_to_all(packed, PEERS, 0, 0, tiled=True)  26.1 us
    all_gather x1, blocking collectives, body(): both = lax.all_gather(pieces, 'core')  2.19 us
    pallas_call x1, Pallas kernels, attend(): pl.pallas_call(lambda *refs: attend_kernel(shards, *refs), name='attend',...  1.99 us

profile of v4, /device:TPU:64, one launch (start us, length us, event | category | flops | bytes accessed | tf_op | source)
XLA Modules:
  0.0 63.4 jit_solution(9582829873065731574)
XLA Ops:
  0.0 2.0 %attend.1 = (f32[144,128]{1,0:T(8,128)S(1)}, bf16[128,8192]{1,0:T(8,128)(2,1)S(1)}) custom-call(s32[8]{0:T(128)} %refs_0_.1, bf16[8,16,128]{2,1,0:T(8,128)(2,1)} %bitcast.15, bf16[8,256,128]{2,1,0:T(8,128)(2,1)} %bitcast.13, bf16[8,256,128]{2,1,0:T(8,128)(2,1)} %bitcast.14, bf16[128,8192]{1,0:T(8,128)(2,1)} %bitcast.12), custom_call_target="tpu_custom_call" | custom-call | tf_op jit(solution)/shard_map/attend/pallas_call | solution.py:78
  2.0 31.8 %all_to_all.10 = f32[144,1,128]{2,1,0:T(1,128)S(1)} all-to-all(f32[144,1,128]{2,1,0:T(1,128)S(1)} %bitcast.11), channel_id=1, replica_groups=mesh['x'=4,'z1'=2,'z0'=2,'y'=4,'core'=2,'rep'=4] {'x','z1','z0'}, dimensions={0} | all-to-all | bytes 147456 | tf_op jit(solution)/shard_map/all_to_all | solution.py:191
  33.7 0.0 copy-start
  33.7 0.5 project.1
  34.2 2.2 %all-gather = f32[128,8,128]{2,1,0:T(8,128)S(1)} all-gather(f32[64,8,128]{2,1,0:T(8,128)S(1)} %project.1), channel_id=2, replica_groups=mesh['x'=4,'z1'=2,'z0'=2,'y'=4,'core'=2,'rep'=4] {'core'}, dimensions={0}, use_global_device_ids=true | all-gather | bytes 786432 | tf_op jit(solution)/shard_map/all_gather | solution.py:201
  36.4 0.1 core_sum.1
  36.6 26.1 %all_to_all.11.got_ref = f32[64,4,128]{2,1,0:T(4,128)S(1)} all-to-all(f32[64,4,128]{2,1,0:T(4,128)S(1)} %core_sum.1), channel_id=1, replica_groups=mesh['x'=4,'z1'=2,'z0'=2,'y'=4,'core'=2,'rep'=4] {'z0','z1','x','y'}, dimensions={0} | all-to-all | bytes 262144 | tf_op jit(solution)/shard_map/all_to_all | solution.py:203
  62.7 0.0 copy-done
  62.7 0.7 %finish.1 = f32[8,64]{1,0:T(8,128)} custom-call(f32[64,4,128]{2,1,0:T(4,128)S(1)} %all_to_all.11.got_ref, f32[8,64]{1,0:T(8,128)S(1)} %copy-done), custom_call_target="tpu_custom_call" | custom-call | tf_op jit(solution)/shard_map/finish/pallas_call | solution.py:169
Async XLA Ops:
  33.7 29.0 %copy-start = (f32[8,64]{1,0:T(8,128)S(1)}, f32[8,64]{1,0:T(8,128)}, u32[]{:S(2)}) copy-start(f32[8,64]{1,0:T(8,128)} %residual_ref.1) | copy-start | bytes 6148

commit v5 on v4

--- a/solution.py
+++ b/solution.py
@@ -10,9 +10,24 @@
 BLOCK_POSITIONS = 32
 LANES = 128
 MEBI = 1 << 20
-SEQ = ("x", "z1", "z0")
-PEERS = ("z0", "z1", "x", "y")
+SEQ = ("x", "z_hi")
 KVH = ("y", "core")
+MESH_AXES = ("x", "z_hi", "y", "core", "rep")
+
+
+def peer_chips(x_size, z_size, y_size):
+    order = (0, 1, 3, 2)
+    planes = (0, 2, 1, 3)
+    chips = [
+        (order[2 * x1 + x0], planes[z], order[2 * y1 + y0])
+        for z in range(4)
+        for x1 in range(2)
+        for y1 in range(2)
+        for x0 in range(2)
+        for y0 in range(2)
+    ]
+    assert (x_size, z_size, y_size) == (4, 4, 4)
+    return chips
 
 
 def attend_kernel(shards, lengths_hbm, query_hbm, key_hbm, value_hbm, matrix_hbm, sent_ref, matrix_ref,
@@ -189,25 +204,30 @@
     )
     lines, size = sent.shape
     got = lax.all_to_all(sent.reshape(lines, 1, size), SEQ, 0, 0, tiled=True).reshape(lines, size)
-    sizes = [lax.axis_size(axis) for axis in PEERS]
+    sizes = [lax.axis_size(axis) for axis in MESH_AXES]
+    chips = peer_chips(*sizes[:3])
+    groups = [
+        [(((x * sizes[1] + z) * sizes[2] + y) * sizes[3] + core) * sizes[4] + rep for x, z, y in chips]
+        for core in range(sizes[3])
+        for rep in range(sizes[4])
+    ]
     places = [
-        ((z0 * sizes[1] + z1) * sizes[2] + x) * sizes[3] + y
-        for x in range(sizes[2])
-        for z1 in range(sizes[1])
-        for z0 in range(sizes[0])
-        for y in range(sizes[3])
+        chips.index((x, z, y))
+        for x in range(sizes[0])
+        for z in range(sizes[1])
+        for y in range(sizes[2])
     ]
     pieces = project(got, matrix, places, rows)
     both = lax.all_gather(pieces, "core")
     packed = core_sum(both)
-    last = lax.all_to_all(packed, PEERS, 0, 0, tiled=True)
+    last = lax.all_to_all(packed, MESH_AXES, 0, 0, axis_index_groups=groups, tiled=True)
     return finish(last, residual)
 
 
 def solution(mesh):
     fine = Mesh(
-        mesh.devices.reshape(4, 2, mesh.shape["seq"] // 8, mesh.shape["kvh"] // 2, 2, mesh.shape["rep"]),
-        ("x", "z1", "z0", "y", "core", "rep"),
+        mesh.devices.reshape(4, mesh.shape["seq"] // 4, mesh.shape["kvh"] // 2, 2, mesh.shape["rep"]),
+        MESH_AXES,
     )
     in_specs = (
         P("rep", KVH, None, None),

time: 63.6 us -> 62.9 us (0.989)
  the two profiles are of different devices: /device:TPU:64 before, /device:TPU:32 now
where the time goes in v5:
time: 62.9 us; the launch traced here: 62.7 us
  blocking collectives  59.4 us (94%)
  Pallas kernels  3.28 us (5%)
    all_to_all x1, blocking collectives, body(): lax.all_to_all(sent.reshape(lines, 1, size), SEQ, 0, 0, tiled=True)  32.7 us
    all_to_all x1, blocking collectives, body(): lax.all_to_all(packed, MESH_AXES, 0, 0, axis_index_groups=groups, tiled=T...  24.5 us
    all_gather x1, blocking collectives, body(): both = lax.all_gather(pieces, 'core')  2.19 us
    pallas_call x1, Pallas kernels, attend(): pl.pallas_call(lambda *refs: attend_kernel(shards, *refs), name='attend',...  1.99 us

profile of v5, /device:TPU:32, one launch (start us, length us, event | category | flops | bytes accessed | tf_op | source)
XLA Modules:
  0.0 62.7 jit_solution(7968057265591175114)
XLA Ops:
  0.0 2.0 %attend.1 = (f32[144,128]{1,0:T(8,128)S(1)}, bf16[128,8192]{1,0:T(8,128)(2,1)S(1)}) custom-call(s32[8]{0:T(128)} %refs_0_.1, bf16[8,16,128]{2,1,0:T(8,128)(2,1)} %bitcast.15, bf16[8,256,128]{2,1,0:T(8,128)(2,1)} %bitcast.13, bf16[8,256,128]{2,1,0:T(8,128)(2,1)} %bitcast.14, bf16[128,8192]{1,0:T(8,128)(2,1)} %bitcast.12), custom_call_target="tpu_custom_call" | custom-call | tf_op jit(solution)/shard_map/attend/pallas_call | solution.py:93
  2.0 32.7 %all_to_all.10 = f32[144,1,128]{2,1,0:T(1,128)S(1)} all-to-all(f32[144,1,128]{2,1,0:T(1,128)S(1)} %bitcast.11), channel_id=1, replica_groups=mesh['x'=4,'z_hi'=4,'y'=4,'core'=2,'rep'=4] {'x','z_hi'}, dimensions={0} | all-to-all | bytes 147456 | tf_op jit(solution)/shard_map/all_to_all | solution.py:206
  34.7 0.0 copy-start
  34.7 0.5 project.1
  35.1 2.2 %all-gather = f32[128,8,128]{2,1,0:T(8,128)S(1)} all-gather(f32[64,8,128]{2,1,0:T(8,128)S(1)} %project.1), channel_id=2, replica_groups=mesh['x'=4,'z_hi'=4,'y'=4,'core'=2,'rep'=4] {'core'}, dimensions={0}, use_global_device_ids=true | all-gather | bytes 786432 | tf_op jit(solution)/shard_map/all_gather | solution.py:221
  37.3 0.1 core_sum.1
  37.5 24.5 %all_to_all.11.got_ref = f32[64,4,128]{2,1,0:T(4,128)S(1)} all-to-all(f32[64,4,128]{2,1,0:T(4,128)S(1)} %core_sum.1), channel_id=1, replica_groups={{0,8,128,136,24,16,152,144,384,392,256,264,408,400,280,272,64,72,192,20..., dimensions={0} | all-to-all | bytes 262144 | tf_op jit(solution)/shard_map/all_to_all | solution.py:223
  62.0 0.0 copy-done
  62.0 0.7 %finish.1 = f32[8,64]{1,0:T(8,128)} custom-call(f32[64,4,128]{2,1,0:T(4,128)S(1)} %all_to_all.11.got_ref, f32[8,64]{1,0:T(8,128)S(1)} %copy-done), custom_call_target="tpu_custom_call" | custom-call | tf_op jit(solution)/shard_map/finish/pallas_call | solution.py:184
Async XLA Ops:
  34.7 27.3 %copy-start = (f32[8,64]{1,0:T(8,128)S(1)}, f32[8,64]{1,0:T(8,128)}, u32[]{:S(2)}) copy-start(f32[8,64]{1,0:T(8,128)} %residual_ref.1) | copy-start | bytes 6148

commit v6 on v5

--- a/solution.py
+++ b/solution.py
@@ -106,15 +106,16 @@
     )(*[pltpu.with_memory_space_constraint(a, pltpu.HBM) for a in operands])
 
 
-def project_kernel(places, got_ref, weight_ref, out_ref):
-    pieces, rows, lanes = out_ref.shape
+def project_kernel(places, got_ref, weight_ref, kept_ref, given_ref):
+    pieces, part, lanes = kept_ref.shape
+    rows = 2 * part
+    half = lanes // 2
     shards = got_ref.shape[0] // (rows + 1)
     logs = got_ref[pl.ds(rows, shards, stride=rows + 1), :]
     factors = jnp.exp(logs - jnp.max(logs, axis=0, keepdims=True))
     factors = factors / jnp.sum(factors, axis=0, keepdims=True)
-    diagonal = lax.broadcasted_iota(jnp.int32, (rows, lanes), 0) == lax.broadcasted_iota(
-        jnp.int32, (rows, lanes), 1
-    )
+    lane = lax.broadcasted_iota(jnp.int32, (rows, lanes), 1)
+    diagonal = lax.broadcasted_iota(jnp.int32, (rows, lanes), 0) == lane
     attended = jnp.zeros((rows, lanes), jnp.float32)
     for s in range(shards):
         factor = jnp.sum(
@@ -122,52 +123,55 @@
         )
         attended += factor * got_ref[pl.ds(s * (rows + 1), rows), :]
     attended = attended.astype(jnp.bfloat16)
+    low = lane[:part] < half
+    first = lax.axis_index("core") == 0
     step = 8
-    for first in range(0, pieces, step):
+    for start in range(0, pieces, step):
         product = jnp.dot(
             attended,
-            weight_ref[:, first * lanes : (first + step) * lanes],
+            weight_ref[:, start * lanes : (start + step) * lanes],
             preferred_element_type=jnp.float32,
         )
         for j in range(step):
-            out_ref[places[first + j]] = product[:, j * lanes : (j + 1) * lanes]
+            piece = product[:, j * lanes : (j + 1) * lanes]
+            turned = pltpu.roll(piece, half, 1)
+            zero = jnp.where(low, piece[:part], turned[part:])
+            one = jnp.where(low, turned[:part], piece[part:])
+            place = places[start + j]
+            kept_ref[place] = jnp.where(first, zero, one)
+            given_ref[place] = jnp.where(first, one, zero)
 
 
 def project(got, weights, places, rows):
     size, features = weights.shape
+    inside = pl.BlockSpec(memory_space=pltpu.VMEM)
+    shape = jax.ShapeDtypeStruct((features // LANES, rows // 2, LANES), jnp.float32)
     return pl.pallas_call(
         lambda *refs: project_kernel(places, *refs),
         name="project",
         compiler_params=pltpu.CompilerParams(vmem_limit_bytes=8 * MEBI),
-        out_shape=jax.ShapeDtypeStruct((features // LANES, rows, LANES), jnp.float32),
-        in_specs=[pl.BlockSpec(memory_space=pltpu.VMEM)] * 2,
-        out_specs=pl.BlockSpec(memory_space=pltpu.VMEM),
+        out_shape=(shape, shape),
+        in_specs=[inside, inside],
+        out_specs=(inside, inside),
     )(got, weights)
 
 
-def core_sum_kernel(got_ref, out_ref):
-    pieces, part, lanes = out_ref.shape
-    half = lanes // 2
-    low = lax.broadcasted_iota(jnp.int32, (part, lanes), 1) < half
+def core_sum_kernel(kept_ref, both_ref, out_ref):
     first = lax.axis_index("core") == 0
-    for i in range(pieces):
-        total = got_ref[0, i] + got_ref[1, i]
-        other = pltpu.roll(total, half, 1)
-        one = jnp.where(first, total, other)
-        two = jnp.where(first, other, total)
-        out_ref[i] = jnp.where(low, one[:part], two[part:])
-
-
-def core_sum(got):
-    cores, pieces, rows, lanes = got.shape
+    for i in range(out_ref.shape[0]):
+        out_ref[i] = kept_ref[i] + jnp.where(first, both_ref[1, i], both_ref[0, i])
+
+
+def core_sum(kept, both):
+    inside = pl.BlockSpec(memory_space=pltpu.VMEM)
     return pl.pallas_call(
         core_sum_kernel,
         name="core_sum",
         compiler_params=pltpu.CompilerParams(vmem_limit_bytes=2 * MEBI),
-        out_shape=jax.ShapeDtypeStruct((pieces, rows // cores, lanes), jnp.float32),
-        in_specs=[pl.BlockSpec(memory_space=pltpu.VMEM)],
-        out_specs=pl.BlockSpec(memory_space=pltpu.VMEM),
-    )(got)
+        out_shape=jax.ShapeDtypeStruct(kept.shape, kept.dtype),
+        in_specs=[inside, inside],
+        out_specs=inside,
+    )(kept, both)
 
 
 def finish_kernel(got_ref, residual_ref, out_ref):
@@ -217,9 +221,8 @@
         for z in range(sizes[1])
         for y in range(sizes[2])
     ]
-    pieces = project(got, matrix, places, rows)
-    both = lax.all_gather(pieces, "core")
-    packed = core_sum(both)
+    kept, given = project(got, matrix, places, rows)
+    packed = core_sum(kept, lax.all_gather(given, "core"))
     last = lax.all_to_all(packed, MESH_AXES, 0, 0, axis_index_groups=groups, tiled=True)
     return finish(last, residual)
 

time: 62.9 us -> 62.9 us (level)
  no operation moved by 1% of the time
where the time goes in v6:
time: 62.9 us; the launch traced here: 62.7 us
  blocking collectives  59.4 us (94%)
  Pallas kernels  3.28 us (5%)
    all_to_all x1, blocking collectives, body(): lax.all_to_all(sent.reshape(lines, 1, size), SEQ, 0, 0, tiled=True)  32.7 us
    all_to_all x1, blocking collectives, body(): lax.all_to_all(packed, MESH_AXES, 0, 0, axis_index_groups=groups, tiled=T...  24.7 us
    all_gather x1, blocking collectives, body(): packed = core_sum(kept, lax.all_gather(given, 'core'))  1.99 us
    pallas_call x1, Pallas kernels, attend(): pl.pallas_call(lambda *refs: attend_kernel(shards, *refs), name='attend',...  1.99 us

profile of v6, /device:TPU:32, one launch (start us, length us, event | category | flops | bytes accessed | tf_op | source)
XLA Modules:
  0.0 62.7 jit_solution(15401092864257672334)
XLA Ops:
  0.0 2.0 %attend.1 = (f32[144,128]{1,0:T(8,128)S(1)}, bf16[128,8192]{1,0:T(8,128)(2,1)S(1)}) custom-call(s32[8]{0:T(128)} %refs_0_.1, bf16[8,16,128]{2,1,0:T(8,128)(2,1)} %bitcast.15, bf16[8,256,128]{2,1,0:T(8,128)(2,1)} %bitcast.13, bf16[8,256,128]{2,1,0:T(8,128)(2,1)} %bitcast.14, bf16[128,8192]{1,0:T(8,128)(2,1)} %bitcast.12), custom_call_target="tpu_custom_call" | custom-call | tf_op jit(solution)/shard_map/attend/pallas_call | solution.py:93
  2.0 0.0 copy-start
  2.0 32.7 %all_to_all.10 = f32[144,1,128]{2,1,0:T(1,128)S(1)} all-to-all(f32[144,1,128]{2,1,0:T(1,128)S(1)} %bitcast.11), channel_id=1, replica_groups=mesh['x'=4,'z_hi'=4,'y'=4,'core'=2,'rep'=4] {'x','z_hi'}, dimensions={0} | all-to-all | bytes 147456 | tf_op jit(solution)/shard_map/all_to_all | solution.py:210
  34.7 0.6 project.1
  35.2 2.0 %all-gather = f32[128,4,128]{2,1,0:T(4,128)S(1)} all-gather(f32[64,4,128]{2,1,0:T(4,128)S(1)} %get-tuple-element.12), channel_id=2, replica_groups=mesh['x'=4,'z_hi'=4,'y'=4,'core'=2,'rep'=4] {'core'}, dimensions={0}, use_global_device_ids=true | all-gather | bytes 393216 | tf_op jit(solution)/shard_map/all_gather | solution.py:225
  37.2 0.1 core_sum.1
  37.3 24.7 %all_to_all.11.got_ref = f32[64,4,128]{2,1,0:T(4,128)S(1)} all-to-all(f32[64,4,128]{2,1,0:T(4,128)S(1)} %core_sum.1), channel_id=1, replica_groups={{0,8,128,136,24,16,152,144,384,392,256,264,408,400,280,272,64,72,192,20..., dimensions={0} | all-to-all | bytes 262144 | tf_op jit(solution)/shard_map/all_to_all | solution.py:226
  62.0 0.0 copy-done
  62.0 0.7 %finish.1 = f32[8,64]{1,0:T(8,128)} custom-call(f32[64,4,128]{2,1,0:T(4,128)S(1)} %all_to_all.11.got_ref, f32[8,64]{1,0:T(8,128)S(1)} %copy-done), custom_call_target="tpu_custom_call" | custom-call | tf_op jit(solution)/shard_map/finish/pallas_call | solution.py:188
Async XLA Ops:
  2.0 60.0 %copy-start = (f32[8,64]{1,0:T(8,128)S(1)}, f32[8,64]{1,0:T(8,128)}, u32[]{:S(2)}) copy-start(f32[8,64]{1,0:T(8,128)} %residual_ref.1) | copy-start | bytes 6148

commit v7 on v5

--- a/solution.py
+++ b/solution.py
@@ -122,7 +122,7 @@
         )
         attended += factor * got_ref[pl.ds(s * (rows + 1), rows), :]
     attended = attended.astype(jnp.bfloat16)
-    step = 8
+    step = 32
     for first in range(0, pieces, step):
         product = jnp.dot(
             attended,

time: 62.9 us -> 62.9 us (level)
  no operation moved by 1% of the time
where the time goes in v7:
time: 62.9 us; the launch traced here: 62.7 us
  blocking collectives  59.4 us (94%)
  Pallas kernels  3.28 us (5%)
    all_to_all x1, blocking collectives, body(): lax.all_to_all(sent.reshape(lines, 1, size), SEQ, 0, 0, tiled=True)  32.7 us
    all_to_all x1, blocking collectives, body(): lax.all_to_all(packed, MESH_AXES, 0, 0, axis_index_groups=groups, tiled=T...  24.5 us
    all_gather x1, blocking collectives, body(): both = lax.all_gather(pieces, 'core')  2.19 us
    pallas_call x1, Pallas kernels, attend(): pl.pallas_call(lambda *refs: attend_kernel(shards, *refs), name='attend',...  1.99 us

profile of v7, /device:TPU:32, one launch (start us, length us, event | category | flops | bytes accessed | tf_op | source)
XLA Modules:
  0.0 62.7 jit_solution(7968057265591175114)
XLA Ops:
  0.0 2.0 %attend.1 = (f32[144,128]{1,0:T(8,128)S(1)}, bf16[128,8192]{1,0:T(8,128)(2,1)S(1)}) custom-call(s32[8]{0:T(128)} %refs_0_.1, bf16[8,16,128]{2,1,0:T(8,128)(2,1)} %bitcast.15, bf16[8,256,128]{2,1,0:T(8,128)(2,1)} %bitcast.13, bf16[8,256,128]{2,1,0:T(8,128)(2,1)} %bitcast.14, bf16[128,8192]{1,0:T(8,128)(2,1)} %bitcast.12), custom_call_target="tpu_custom_call" | custom-call | tf_op jit(solution)/shard_map/attend/pallas_call | solution.py:93
  2.0 32.7 %all_to_all.10 = f32[144,1,128]{2,1,0:T(1,128)S(1)} all-to-all(f32[144,1,128]{2,1,0:T(1,128)S(1)} %bitcast.11), channel_id=1, replica_groups=mesh['x'=4,'z_hi'=4,'y'=4,'core'=2,'rep'=4] {'x','z_hi'}, dimensions={0} | all-to-all | bytes 147456 | tf_op jit(solution)/shard_map/all_to_all | solution.py:206
  34.7 0.0 copy-start
  34.7 0.5 project.1
  35.1 2.2 %all-gather = f32[128,8,128]{2,1,0:T(8,128)S(1)} all-gather(f32[64,8,128]{2,1,0:T(8,128)S(1)} %project.1), channel_id=2, replica_groups=mesh['x'=4,'z_hi'=4,'y'=4,'core'=2,'rep'=4] {'core'}, dimensions={0}, use_global_device_ids=true | all-gather | bytes 786432 | tf_op jit(solution)/shard_map/all_gather | solution.py:221
  37.3 0.1 core_sum.1
  37.5 24.5 %all_to_all.11.got_ref = f32[64,4,128]{2,1,0:T(4,128)S(1)} all-to-all(f32[64,4,128]{2,1,0:T(4,128)S(1)} %core_sum.1), channel_id=1, replica_groups={{0,8,128,136,24,16,152,144,384,392,256,264,408,400,280,272,64,72,192,20..., dimensions={0} | all-to-all | bytes 262144 | tf_op jit(solution)/shard_map/all_to_all | solution.py:223
  62.0 0.0 copy-done
  62.0 0.7 %finish.1 = f32[8,64]{1,0:T(8,128)} custom-call(f32[64,4,128]{2,1,0:T(4,128)S(1)} %all_to_all.11.got_ref, f32[8,64]{1,0:T(8,128)S(1)} %copy-done), custom_call_target="tpu_custom_call" | custom-call | tf_op jit(solution)/shard_map/finish/pallas_call | solution.py:184
Async XLA Ops:
  34.7 27.3 %copy-start = (f32[8,64]{1,0:T(8,128)S(1)}, f32[8,64]{1,0:T(8,128)}, u32[]{:S(2)}) copy-start(f32[8,64]{1,0:T(8,128)} %residual_ref.1) | copy-start | bytes 6148
